TPU v7x, 32 devices: a whole 2x2x4 slice. The times are simulated.
32 devices in a mesh: hid: 8 (over y, x, core), ep: 4 (over z).
Axes of the slice: x: 2, y: 2, z: 4, core: 2. Of those that a mesh axis runs over, the one named last changes fastest.
Arguments:
- tokens: bfloat16 [2048, 2048], P('ep', 'hid'), may hold values from -6 to 6
- expert_ids: int32 [2048, 6], P('ep'), may hold values from 0 to 15, all different within a row; in each aligned block of 512 rows (0 to 511, 512 to 1023, ...) at most 256 rows name the same one
- gate_weights: float32 [2048, 6], P('ep'), may hold values from 0.1 to 1
- w_gate_up: bfloat16 [4, 5632, 2, 2048], P('ep', 'hid'), may hold values from -0.125 to 0.125
- w_down: bfloat16 [4, 5632, 2048], P('ep', 'hid'), may hold values from -0.21875 to 0.21875
Outputs:
- mixed: bfloat16 [2048, 2048], P('ep', 'hid')
Inputs may be any that keep to these rules, and one draw needn't show every extreme that they name: `expert_ids`: the 6 ids of a row differ. Among the 512 rows of one index of ep (aligned blocks of rows), no expert is named by more than 256 rows.
All inputs are finite; a program needn't handle non-finite values.
Results may differ from a plain program's by a relative error of at most 0.0064.
Values may be sent and summed in bfloat16 or wider, within the bound.
A program may use at most 64 MiB of HBM per device.

v0:
```python
import jax
import jax.numpy as jnp
from jax import lax
from jax.sharding import PartitionSpec as P

EXP_DEV = 4


def slot_numbers(ids, count):
    flat = ids.reshape(-1)
    onehot = (flat[:, None] == jnp.arange(count, dtype=jnp.int32)[None, :]).astype(jnp.int32)
    before = jnp.cumsum(onehot, axis=0) - onehot
    return jnp.sum(before * onehot, axis=1).reshape(ids.shape)


def on_device(tokens, expert_ids, gate_weights, w_gate_up, w_down):
    groups = lax.axis_size("ep")
    hid_count = lax.axis_size("hid")
    shards = hid_count // EXP_DEV
    experts = EXP_DEV * groups
    tok_rows = tokens.shape[0]
    width_local = tokens.shape[1]
    topk = expert_ids.shape[1]
    capacity = tok_rows * topk * 4 // (3 * experts)
    rows_per = groups * capacity
    slot = slot_numbers(expert_ids, experts)
    token_index = jnp.broadcast_to(jnp.arange(tok_rows, dtype=jnp.int32)[:, None], expert_ids.shape)
    table = (
        jnp.full((experts, capacity), tok_rows, dtype=jnp.int32)
        .at[expert_ids, slot]
        .set(token_index)
    )
    padded = jnp.concatenate([tokens, jnp.zeros((1, width_local), tokens.dtype)], axis=0)
    placed = padded[table].reshape(groups, EXP_DEV, capacity, width_local)
    arrived = lax.all_to_all(placed, "ep", split_axis=0, concat_axis=2, tiled=True)[0]
    repeated = jnp.repeat(arrived, shards, axis=0)
    outgoing = jnp.transpose(repeated, (1, 0, 2)).reshape(rows_per, hid_count * width_local)
    full_rows = lax.all_to_all(outgoing, "hid", split_axis=1, concat_axis=1, tiled=True)
    gate_up = jnp.einsum("rd,fgd->gfr", full_rows, w_gate_up[0], preferred_element_type=jnp.float32)
    hidden = (jax.nn.silu(gate_up[0]) * gate_up[1]).astype(jnp.bfloat16)
    partial_value = jnp.einsum("fr,fd->rd", hidden, w_down[0], preferred_element_type=jnp.float32)
    rounded = partial_value.astype(jnp.bfloat16)
    homed = lax.all_to_all(
        rounded.reshape(1, groups, capacity, rounded.shape[1]),
        "ep",
        split_axis=1,
        concat_axis=0,
        tiled=True,
    )
    moved = lax.all_to_all(homed, "hid", split_axis=3, concat_axis=0, tiled=True)
    grouped = moved.reshape(EXP_DEV, shards, groups, capacity, width_local).astype(jnp.float32)
    summed = jnp.sum(grouped, axis=1).astype(jnp.bfloat16)
    back = jnp.transpose(summed, (1, 0, 2, 3))
    flat = back.reshape(experts * capacity, width_local)
    picked = flat[expert_ids * capacity + slot]
    mixed = jnp.sum(picked.astype(jnp.float32) * gate_weights[:, :, None], axis=1)
    return mixed.astype(jnp.bfloat16)


def solution(mesh):
    return jax.shard_map(
        on_device,
        mesh=mesh,
        in_specs=(
            P("ep", "hid"),
            P("ep", None),
            P("ep", None),
            P("ep", "hid", None, None),
            P("ep", "hid", None),
        ),
        out_specs=P("ep", "hid"),
        check_vma=False,
    )
```

profile of v0, /device:TPU:0, one launch (start us, length us, event | category | flops | bytes accessed | tf_op | source)
XLA Modules:
  0.0 363.1 jit_solution(8262749961850203869)
XLA Ops:
  0.0 1.0 copy.60
  1.4 4.6 %reduce-window.6 = s32[16,24,128]{2,1,0:T(8,128)S(1)} reduce-window(s32[16,24,128]{2,1,0:T(8,128)S(1)} %fusion.12, s32[]{:T(128)} %constant.5.clone.1), window={size=1x1x128 pad=0_0x0_0x127_0}, to_apply=%region_0.0 | reduce-window | flops 6242304 | bytes 393220 | tf_op jit(solution)/shard_map/reduce-window
  6.0 0.4 slice_reduce_fusion
  6.8 0.2 reshape.83
  7.0 0.2 reshape.77
  8.3 11.8 %scatter_custom_fusion = s32[4096]{0:T(1024)S(1)} fusion(s32[3072]{0:T(1024)S(1)} %reshape.104, s32[3072]{0:T(1024)S(1)} %reshape.106, s32[]{:T(128)} %constant.10.clone.1), kind=kCustom, calls=%fused_computation.31 | custom fusion | bytes 16388
  20.2 1.0 concatenate.6
  21.2 16.9 %gather_fusion = bf16[4096,256]{1,0:T(8,128)(2,1)} fusion(bf16[513,256]{1,0:T(8,128)(2,1)S(1)} %concatenate.6, s32[4096]{0:T(1024)S(1)} %broadcast_clamp_fusion), kind=kCustom, calls=%fused_computation | custom fusion | bytes 4210688 | tf_op jit(solution)/shard_map/gather | solution.py:34
  38.1 54.5 %all_to_all.51 = bf16[4,4,256,256]{3,2,1,0:T(8,128)(2,1)S(1)} all-to-all(bf16[4,4,256,256]{3,2,1,0:T(8,128)(2,1)} %bitcast.59), channel_id=1, replica_groups=mesh['hid'=8,'ep'=4] {'ep'}, dimensions={0} | all-to-all | bytes 4194304 | tf_op jit(solution)/shard_map/all_to_all | solution.py:35
  92.8 0.3 broadcast_in_dim.29
  93.1 52.6 %all_to_all.52 = bf16[1024,8,256]{2,0,1:T(8,128)(2,1)S(1)} all-to-all(bf16[1024,8,256]{2,0,1:T(8,128)(2,1)S(1)} %bitcast.55), channel_id=1, replica_groups=mesh['hid'=8,'ep'=4] {'hid'}, dimensions={1} | all-to-all | bytes 8388608 | tf_op jit(solution)/shard_map/all_to_all | solution.py:38
  145.6 4.3 %copy.66 = bf16[1024,8,256]{2,1,0:T(8,128)(2,1)} copy(bf16[1024,8,256]{2,0,1:T(8,128)(2,1)S(1)} %all_to_all.52) | data formatting | bytes 8388608 | tf_op jit(solution)/shard_map/all_to_all | solution.py:38
  150.0 7.4 %reshape.116 = bf16[1024,2048,1]{1,0,2:T(8,128)(2,1)} reshape(bf16[1024,8,256]{2,1,0:T(8,128)(2,1)} %copy.66) | data formatting | bytes 8388608 | tf_op jit(solution)/shard_map/all_to_all | solution.py:38
  157.4 12.0 %fusion.4 = f32[2,704,1024]{2,1,0:T(8,128)S(1)} fusion(bf16[1024,2048,1]{1,0,2:T(8,128)(2,1)} %reshape.116, bf16[704,2,2048]{2,1,0:T(2,128)(2,1)} %bitcast.64), kind=kOutput, calls=%fused_computation.10 | convolution fusion | flops 5905580032 | bytes 15728640 | tf_op jit(solution)/shard_map/rd,fgd->gfr/dot_general | solution.py:39
  169.4 3.9 %convolution_convert_fusion = bf16[1024,2048]{1,0:T(8,128)(2,1)S(1)} fusion(bf16[1,704,2048]{2,1,0:T(8,128)(2,1)S(1)} %copy-done, f32[2,704,1024]{2,1,0:T(8,128)S(1)} %fusion.4), kind=kOutput, calls=%fused_computation.6 | convolution fusion | flops 2959212544 | bytes 12845056 | tf_op jit(solution)/shard_map/fr,fd->rd/dot_general | solution.py:41
  173.3 96.3 %all_to_all.53 = bf16[1,4,256,2048]{3,2,0,1:T(8,128)(2,1)} all-to-all(bf16[1,4,256,2048]{3,2,0,1:T(8,128)(2,1)S(1)} %bitcast.60), channel_id=1, replica_groups=mesh['hid'=8,'ep'=4] {'ep'}, dimensions={1} | all-to-all | bytes 8388608 | tf_op jit(solution)/shard_map/all_to_all | solution.py:43
  269.6 7.5 %copy.69 = bf16[4,1,256,2048]{2,0,1,3:T(4,128)(2,1)} copy(bf16[4,1,256,2048]{3,2,0,1:T(8,128)(2,1)} %bitcast.56) | data formatting | bytes 8388608 | tf_op jit(solution)/shard_map/all_to_all | solution.py:43
  277.1 4.9 %all-to-all-start.3 = ((bf16[4,1,256,2048]{2,0,1,3:T(4,128)(2,1)}), bf16[4,1,256,2048]{2,0,1,3:T(4,128)(2,1)}, u32[]{:S(2)}, u32[]{:S(2)}) async-start(bf16[4,1,256,2048]{2,0,1,3:T(4,128)(2,1)} %copy.69), calls=%async_computation.3 | async-start | bytes 8388608 | tf_op jit(solution)/shard_map/all_to_all | solution.py:50
  282.5 48.4 %all-to-all-done.3 = bf16[4,1,256,2048]{2,0,1,3:T(4,128)(2,1)} async-done(((bf16[4,1,256,2048]{2,0,1,3:T(4,128)(2,1)}), bf16[4,1,256,2048]{2,0,1,3:T(4,128)(2,1)}, u32[]{:S(2)}, u32[]{:S(2)}) %all-to-all-start.3) | async-done | bytes 4194336 | tf_op jit(solution)/shard_map/all_to_all | solution.py:50
  330.9 6.9 %reduce_sum.31 = bf16[4,4,256,256]{2,1,3,0:T(4,128)(2,1)} reduce(bf16[4,2,4,256,256]{3,2,4,1,0:T(4,128)(2,1)} %bitcast.17, bf16[]{:T(256)} %constant.9.clone.1), dimensions={1}, to_apply=%region_4.5 | reduce | flops 1048576 | bytes 6291458 | tf_op jit(solution)/shard_map/reduce_sum | solution.py:52
  337.8 3.0 copy.71
  340.8 13.0 %gather_fusion.1 = bf16[3072,256]{1,0:T(8,128)(2,1)} fusion(bf16[4096,256]{1,0:T(8,128)(2,1)S(1)} %bitcast.54, s32[3072]{0:T(1024)S(1)} %broadcast_clamp_fusion.1), kind=kCustom, calls=%fused_computation.1 | custom fusion | bytes 3158016 | tf_op jit(solution)/shard_map/gather | solution.py:55
  353.8 4.1 %reshape.115 = f32[512,6,256]{2,1,0:T(8,128)} reshape(bf16[3072,256]{1,0:T(8,128)(2,1)} %gather_fusion.1) | data formatting | bytes 4718592 | tf_op jit(solution)/shard_map/convert_element_type | solution.py:56
  357.9 5.2 %multiply_reduce_fusion = bf16[512,256]{1,0:T(8,128)(2,1)} fusion(f32[512,6,256]{2,1,0:T(8,128)} %reshape.115, f32[512,6]{1,0:T(8,128)S(1)} %copy.74), kind=kLoop, calls=%fused_computation.5 | loop fusion | flops 1441792 | bytes 3420160 | tf_op jit(solution)/shard_map/reduce_sum | solution.py:56
  (39 shorter events, 2.4 us)
Async XLA Ops:
  0.0 169.4 %copy-start = (bf16[1,704,2048]{2,1,0:T(8,128)(2,1)S(1)}, bf16[1,704,2048]{2,1,0:T(8,128)(2,1)}, u32[]{:S(2)}) copy-start(bf16[1,704,2048]{2,1,0:T(8,128)(2,1)} %param.9) | copy-start | bytes 8650756
  0.0 7.6 %copy-start.5 = (s32[2]{0:T(128)S(1)}, s32[2]{0:T(128)}, u32[]{:S(2)}) copy-start(s32[2]{0:T(128)} %constant.30) | copy-start | bytes 28
  0.0 7.7 %copy-start.4 = (s32[2]{0:T(128)S(1)}, s32[2]{0:T(128)}, u32[]{:S(2)}) copy-start(s32[2]{0:T(128)} %constant.33) | copy-start | bytes 28
  0.0 7.4 %copy-start.2 = (s32[512,6]{0,1:T(8,128)S(1)}, s32[512,6]{0,1:T(8,128)}, u32[]{:S(2)}) copy-start(s32[512,6]{0,1:T(8,128)} %param.6) | copy-start | bytes 36868
  277.1 5.2 %copy-start.3 = (f32[512,6]{0,1:T(8,128)S(1)}, f32[512,6]{0,1:T(8,128)}, u32[]{:S(2)}) copy-start(f32[512,6]{0,1:T(8,128)} %param.7) | copy-start | bytes 36868
  277.1 53.8 %all-to-all-start.3 = ((bf16[4,1,256,2048]{2,0,1,3:T(4,128)(2,1)}), bf16[4,1,256,2048]{2,0,1,3:T(4,128)(2,1)}, u32[]{:S(2)}, u32[]{:S(2)}) async-start(bf16[4,1,256,2048]{2,0,1,3:T(4,128)(2,1)} %copy.69), calls=%async_computation.3 | async-start | bytes 8388608 | tf_op jit(solution)/shard_map/all_to_all | solution.py:50
  353.8 9.3 %copy-start.1 = (bf16[1,704,2048]{2,1,0:T(8,128)(2,1)S(1)}, bf16[1,704,2048]{2,1,0:T(8,128)(2,1)}, u32[]{:S(2)}) copy-start(bf16[1,704,2048]{2,1,0:T(8,128)(2,1)} %param.9) | copy-start | bytes 8650756
where the time goes:
time: 364 us; the launch traced here: 363 us
  blocking collectives  203 us (56%)
  local copies, waits for them, and re-layouts  72.8 us (20%)
  waiting for transfers between devices  48.4 us (13%)
  other arithmetic  17.4 us (5%)
  matrix products  15.9 us (4%)
  starting transfers between devices  4.9 us (1%)
    all_to_all x1, blocking collectives, on_device(): lax.all_to_all(rounded.reshape(1, groups, capacity, rounded.shape[1]), 'e...  96.3 us
    all_to_all x1, blocking collectives, on_device(): lax.all_to_all(placed, 'ep', split_axis=0, concat_axis=2, tiled=True)[0]  54.5 us
    all_to_all x1, blocking collectives, on_device(): lax.all_to_all(outgoing, 'hid', split_axis=1, concat_axis=1, tiled=True)  52.6 us
    all_to_all x1, waiting for transfers between devices, on_device(): lax.all_to_all(homed, 'hid', split_axis=3, concat_axis=0, tiled=True)  48.4 us
    gather x1, local copies, waits for them, and re-layouts, on_device(): placed = padded[table].reshape(groups, EXP_DEV, capacity, width_local)  16.9 us
    unnamed x18, local copies, waits for them, and re-layouts  13.3 us
    gather x1, local copies, waits for them, and re-layouts, on_device(): picked = flat[expert_ids * capacity + slot]  13 us
    dot_general x1, matrix products, on_device(): jnp.einsum('rd,fgd->gfr', full_rows, w_gate_up[0], preferred_element_type...  12 us
  transfers between devices with their start and end apart: 1, of which 1 were waited for; matrix products, arithmetic and copies ran while one was open for 0% of the time, Pallas kernels for 0%

commit v1 on v0

--- a/solution.py
+++ b/solution.py
@@ -1,9 +1,325 @@
+import functools
+
 import jax
 import jax.numpy as jnp
 from jax import lax
+from jax.experimental import pallas as pl
+from jax.experimental.pallas import tpu as pltpu
 from jax.sharding import PartitionSpec as P
 
 EXP_DEV = 4
+MESH = pl.DeviceIdType.MESH
+
+
+def partner_at(me, step, count):
+    if count & (count - 1):
+        return lax.rem(me + step, count)
+    found, bit = 0, 1
+    while bit < count:
+        found = found + (((me // bit) % 2 + (step // bit) % 2) % 2) * bit
+        bit *= 2
+    return found
+
+
+def layer_kernel(
+    groups, hid_count, capacity,
+    tok_ref, ids_ref, gates_ref, up_hbm, down_hbm, out_ref,
+    w_pair, w_gate, w_up, w_down, meta, meta_in, x_all, r_send, rows,
+    p_buf, p_in, y_send, y_in, z_send, z_in, own,
+    load_sem, tok_ss, tok_rs, meta_ss, meta_rs, row_ss, row_rs, keep_sem,
+    fwd_ss, fwd_rs, part_ss, part_rs, y_ss, y_rs, z_ss, z_rs,
+):
+    shards = hid_count // EXP_DEV
+    tok_rows, width = tok_ref.shape
+    experts = EXP_DEV * groups
+    ep = lax.axis_index("ep")
+    hid = lax.axis_index("hid")
+    mine = hid // shards
+    core = hid % shards
+
+    def place(h):
+        return pl.ds(pl.multiple_of(h * width, 128), width)
+
+    def at(e, c):
+        return e * shards + c
+
+    def z_dev(g):
+        return {"ep": g, "hid": hid}
+
+    def h_dev(h):
+        return {"ep": ep, "hid": h}
+
+    def remote(src, dst, ss, rs, dev):
+        return pltpu.make_async_remote_copy(
+            src_ref=src, dst_ref=dst, send_sem=ss, recv_sem=rs, device_id=dev, device_id_type=MESH
+        )
+
+    load_up = pltpu.make_async_copy(up_hbm, w_pair, load_sem.at[0])
+    load_down = pltpu.make_async_copy(down_hbm, w_down, load_sem.at[1])
+    load_up.start()
+    load_down.start()
+
+    barrier = pltpu.get_barrier_semaphore()
+    peers = [z_dev(partner_at(ep, s, groups)) for s in range(1, groups)]
+    peers += [h_dev(at((mine + k) % EXP_DEV, core)) for k in range(1, EXP_DEV)]
+    peers += [h_dev(at(mine, (core + j) % shards)) for j in range(1, shards)]
+    for dev in peers:
+        pl.semaphore_signal(barrier, inc=1, device_id=dev, device_id_type=MESH)
+
+    eid = lax.broadcasted_iota(jnp.int32, (experts, tok_rows), 0)
+    hit = jnp.zeros((experts, tok_rows), jnp.float32)
+    gate = jnp.zeros((experts, tok_rows), jnp.float32)
+    for k in range(ids_ref.shape[0]):
+        same = ids_ref[k : k + 1, :] == eid
+        hit = hit + jnp.where(same, 1.0, 0.0)
+        gate = gate + jnp.where(same, gates_ref[k : k + 1, :], 0.0)
+    earlier = lax.broadcasted_iota(jnp.int32, (tok_rows, tok_rows), 0) < lax.broadcasted_iota(
+        jnp.int32, (tok_rows, tok_rows), 1
+    )
+    before = jnp.dot(
+        hit.astype(jnp.bfloat16),
+        jnp.where(earlier, 1.0, 0.0).astype(jnp.bfloat16),
+        preferred_element_type=jnp.float32,
+    )
+    slot = jnp.where(hit > 0.5, before, -1.0)
+    for g in range(groups):
+        meta[g, 0:EXP_DEV] = slot[g * EXP_DEV : (g + 1) * EXP_DEV]
+        meta[g, EXP_DEV : 2 * EXP_DEV] = gate[g * EXP_DEV : (g + 1) * EXP_DEV]
+
+    pl.semaphore_wait(barrier, len(peers))
+
+    def tok_copy(s):
+        g = partner_at(ep, s, groups)
+        return remote(tok_ref, x_all.at[ep], tok_ss.at[s], tok_rs.at[s], z_dev(g))
+
+    def meta_copy(s):
+        g = partner_at(ep, s, groups)
+        return remote(meta.at[g], meta_in.at[ep], meta_ss.at[s], meta_rs.at[s], z_dev(g))
+
+    for s in range(1, groups):
+        meta_copy(s).start()
+        tok_copy(s).start()
+    x_all[ep] = tok_ref[...]
+    meta_in[ep] = meta[ep]
+
+    load_up.wait()
+    load_down.wait()
+    step_rows = 16
+
+    def split(i, carry):
+        r = pl.ds(pl.multiple_of(i * step_rows, step_rows), step_rows)
+        w_gate[r, :] = w_pair[r, 0, :]
+        w_up[r, :] = w_pair[r, 1, :]
+        return carry
+
+    lax.fori_loop(0, w_gate.shape[0] // step_rows, split, 0)
+
+    def row_copy(b, k):
+        e = (mine + k) % EXP_DEV
+        return remote(r_send.at[b, e], rows.at[b, :, place(hid)], row_ss.at[b, k], row_rs.at[b, k], h_dev(at(e, core)))
+
+    def keep_copy(b):
+        return pltpu.make_async_copy(r_send.at[b, mine], rows.at[b, :, place(hid)], keep_sem.at[b])
+
+    def fwd_copy(b, k, j):
+        other = h_dev(at(mine, (core + j) % shards))
+        h = at((mine + EXP_DEV - k) % EXP_DEV, core)
+        src = r_send.at[b, mine] if k == 0 else rows.at[b, :, place(h)]
+        return remote(src, rows.at[b, :, place(h)], fwd_ss.at[b, k, j], fwd_rs.at[b, k, j], other)
+
+    def part_copy(b, j):
+        c = (core + j) % shards
+        return remote(p_buf.at[b, c], p_in.at[b, j], part_ss.at[b, j], part_rs.at[b, j], h_dev(at(mine, c)))
+
+    def y_copy(b, k):
+        e = (mine + k) % EXP_DEV
+        return remote(y_send.at[b, e], y_in.at[b, mine], y_ss.at[b, k], y_rs.at[b, k], h_dev(at(e, core)))
+
+    def z_copy(s):
+        g = partner_at(ep, s, groups)
+        return remote(z_send.at[s], z_in.at[s], z_ss.at[s], z_rs.at[s], z_dev(g))
+
+    slot_id = lax.broadcasted_iota(jnp.int32, (capacity, tok_rows), 0).astype(jnp.float32)
+
+    def stage_rows(s):
+        b = partner_at(ep, s, groups)
+
+        @pl.when(s > 0)
+        def _():
+            meta_copy(s).wait_recv()
+            tok_copy(s).wait_recv()
+
+        x = x_all[b]
+        for e in range(EXP_DEV):
+            pick = jnp.where(meta_in[b, e : e + 1, :] == slot_id, 1.0, 0.0).astype(jnp.bfloat16)
+            r_send[b, e] = jnp.dot(pick, x, preferred_element_type=jnp.float32).astype(jnp.bfloat16)
+        for k in (2, 1, 3):
+            row_copy(b, k).start()
+        keep_copy(b).start()
+        for j in range(1, shards):
+            fwd_copy(b, 0, j).start()
+
+    def stage_forward(s):
+        b = partner_at(ep, s, groups)
+        for k in (1, 3, 2):
+            row_from(b, k).wait_recv()
+            for j in range(1, shards):
+                fwd_copy(b, k, j).start()
+
+    def stage_experts(s):
+        b = partner_at(ep, s, groups)
+        keep_copy(b).wait()
+        for k in range(EXP_DEV):
+            for j in range(1, shards):
+                fwd_copy(b, k, j).wait_recv()
+        x = rows[b]
+        nt = (((1,), (1,)), ((), ()))
+        gate = lax.dot_general(x, w_gate[...], nt, preferred_element_type=jnp.float32)
+        up = lax.dot_general(x, w_up[...], nt, preferred_element_type=jnp.float32)
+        hidden = (gate / (1.0 + jnp.exp(-gate)) * up).astype(jnp.bfloat16)
+        for c in range(shards):
+            for e in range(EXP_DEV):
+                cols = slice(at(e, c) * width, (at(e, c) + 1) * width)
+                p_buf[b, c, e] = jnp.dot(
+                    hidden, w_down[:, cols], preferred_element_type=jnp.float32
+                ).astype(jnp.bfloat16)
+        for j in range(1, shards):
+            part_copy(b, j).start()
+
+    def stage_sum(s):
+        b = partner_at(ep, s, groups)
+        for j in range(1, shards):
+            part_copy(b, j).wait_recv()
+        for e in range(EXP_DEV):
+            y = p_buf[b, core, e].astype(jnp.float32)
+            for j in range(1, shards):
+                y = y + p_in[b, j, e].astype(jnp.float32)
+            y_send[b, e] = y.astype(jnp.bfloat16)
+        for k in (2, 1, 3):
+            y_copy(b, k).start()
+        y_in[b, mine] = y_send[b, mine]
+
+    def stage_mix(s):
+        b = partner_at(ep, s, groups)
+        for k in (1, 3, 2):
+            y_from(b, k).wait_recv()
+        total = jnp.zeros((tok_rows, width), jnp.float32)
+        for e in range(EXP_DEV):
+            spread = jnp.where(
+                meta_in[b, e : e + 1, :] == slot_id, meta_in[b, EXP_DEV + e : EXP_DEV + e + 1, :], 0.0
+            ).astype(jnp.bfloat16)
+            total = total + lax.dot_general(
+                spread, y_in[b, e], (((0,), (0,)), ((), ())), preferred_element_type=jnp.float32
+            )
+
+        @pl.when(s == 0)
+        def _():
+            own[...] = total
+
+        @pl.when(s > 0)
+        def _():
+            z_send[s] = total.astype(jnp.bfloat16)
+            z_copy(s).start()
+
+    def y_from(b, k):
+        e = (mine + EXP_DEV - k) % EXP_DEV
+        return remote(y_send.at[b, e], y_in.at[b, e], y_ss.at[b, k], y_rs.at[b, k], h_dev(at(e, core)))
+
+    def row_from(b, k):
+        e = (mine + EXP_DEV - k) % EXP_DEV
+        return remote(r_send.at[b, e], rows.at[b, :, place(at(e, core))], row_ss.at[b, k], row_rs.at[b, k], h_dev(at(e, core)))
+
+    def tick(t, carry):
+        for lag, stage in ((0, stage_rows), (1, stage_forward), (3, stage_sum), (4, stage_mix), (2, stage_experts)):
+            s = t - lag
+
+            @pl.when((s >= 0) & (s < groups))
+            def _():
+                stage(s)
+
+        return carry
+
+    lax.fori_loop(0, groups + 4, tick, 0)
+
+    total = own[...]
+    for s in range(1, groups):
+        z_copy(s).wait_recv()
+        total = total + z_in[s].astype(jnp.float32)
+    out_ref[...] = total.astype(out_ref.dtype)
+
+    for s in range(1, groups):
+        meta_copy(s).wait_send()
+        tok_copy(s).wait_send()
+        z_copy(s).wait_send()
+
+    def drain(b, carry):
+        for k in range(1, EXP_DEV):
+            row_copy(b, k).wait_send()
+            y_copy(b, k).wait_send()
+        for j in range(1, shards):
+            part_copy(b, j).wait_send()
+            for k in range(EXP_DEV):
+                fwd_copy(b, k, j).wait_send()
+        return carry
+
+    lax.fori_loop(0, groups, drain, 0)
+
+
+def fused_layer(tokens, expert_ids, gate_weights, w_gate_up, w_down):
+    groups = lax.axis_size("ep")
+    hid_count = lax.axis_size("hid")
+    shards = hid_count // EXP_DEV
+    tok_rows, width = tokens.shape
+    topk = expert_ids.shape[1]
+    capacity = tok_rows * topk * 4 // (3 * EXP_DEV * groups)
+    units, _, depth = w_gate_up.shape[1:]
+    bf, dma = jnp.bfloat16, pltpu.SemaphoreType.DMA
+    vmem = pl.BlockSpec(memory_space=pltpu.VMEM)
+    hbm = pl.BlockSpec(memory_space=pl.ANY)
+    block = (capacity, width)
+    return pl.pallas_call(
+        functools.partial(layer_kernel, groups, hid_count, capacity),
+        out_shape=jax.ShapeDtypeStruct((tok_rows, width), bf),
+        in_specs=[vmem, vmem, vmem, hbm, hbm],
+        out_specs=vmem,
+        scratch_shapes=[
+            pltpu.VMEM((units, 2, depth), bf),
+            pltpu.VMEM((units, depth), bf),
+            pltpu.VMEM((units, depth), bf),
+            pltpu.VMEM((units, depth), bf),
+            pltpu.VMEM((groups, 2 * EXP_DEV, tok_rows), jnp.float32),
+            pltpu.VMEM((groups, 2 * EXP_DEV, tok_rows), jnp.float32),
+            pltpu.VMEM((groups, tok_rows, width), bf),
+            pltpu.VMEM((groups, EXP_DEV) + block, bf),
+            pltpu.VMEM((groups, capacity, depth), bf),
+            pltpu.VMEM((groups, shards, EXP_DEV) + block, bf),
+            pltpu.VMEM((groups, shards, EXP_DEV) + block, bf),
+            pltpu.VMEM((groups, EXP_DEV) + block, bf),
+            pltpu.VMEM((groups, EXP_DEV) + block, bf),
+            pltpu.VMEM((groups, tok_rows, width), bf),
+            pltpu.VMEM((groups, tok_rows, width), bf),
+            pltpu.VMEM((tok_rows, width), jnp.float32),
+            dma((2,)),
+            dma((groups,)),
+            dma((groups,)),
+            dma((groups,)),
+            dma((groups,)),
+            dma((groups, EXP_DEV)),
+            dma((groups, EXP_DEV)),
+            dma((groups,)),
+            dma((groups, EXP_DEV, shards)),
+            dma((groups, EXP_DEV, shards)),
+            dma((groups, shards)),
+            dma((groups, shards)),
+            dma((groups, EXP_DEV)),
+            dma((groups, EXP_DEV)),
+            dma((groups,)),
+            dma((groups,)),
+        ],
+        compiler_params=pltpu.CompilerParams(
+            collective_id=0, has_side_effects=True, vmem_limit_bytes=60 * 1024 * 1024
+        ),
+    )(tokens, expert_ids.T, gate_weights.T, w_gate_up[0], w_down[0])
 
 
 def slot_numbers(ids, count):
@@ -58,8 +374,12 @@
 
 
 def solution(mesh):
+    def layer(tokens, *rest):
+        fits = tokens.shape[1] % 128 == 0
+        return (fused_layer if fits else on_device)(tokens, *rest)
+
     return jax.shard_map(
-        on_device,
+        layer,
         mesh=mesh,
         in_specs=(
             P("ep", "hid"),

time: 364 us -> 92 us (0.25)
  the two profiles are of different devices: /device:TPU:0 before, /device:TPU:9 now
where the time goes in v1:
time: 92 us; the launch traced here: 91.9 us
  Pallas kernels  90.2 us (98%)
  local copies, waits for them, and re-layouts  1.67 us (2%)
    pallas_call x1, Pallas kernels, fused_layer(): pl.pallas_call(functools.partial(layer_kernel, groups, hid_count, capacit...  90.2 us

profile of v1, /device:TPU:9, one launch (start us, length us, event | category | flops | bytes accessed | tf_op | source)
XLA Modules:
  0.0 91.9 jit_solution(14847733471310970664)
XLA Ops:
  0.0 90.2 %shard_map.55 = bf16[512,256]{1,0:T(8,128)(2,1)} custom-call(bf16[512,256]{1,0:T(8,128)(2,1)} %tok_ref.1, s32[6,512]{1,0:T(8,128)} %bitcast.6, f32[6,512]{1,0:T(8,128)} %bitcast.7, bf16[704,2,2048]{2,1,0:T(2,128)(2,1)} %bitcast.4, bf16[704,2048]{1,0:T(8,128)(2,1)} %bitcast.5), custom_call_target="tpu_custom_call" | custom-call | tf_op jit(solution)/shard_map/pallas_call | solution.py:280
  90.2 1.7 %copy.7 = bf16[512,256]{1,0:T(8,128)(2,1)} copy(bf16[512,256]{1,0:T(8,128)(2,1)} %shard_map.55) | data formatting | bytes 524288

commit v2 on v1

--- a/solution.py
+++ b/solution.py
@@ -11,14 +11,14 @@
 MESH = pl.DeviceIdType.MESH
 
 
-def partner_at(me, step, count):
-    if count & (count - 1):
-        return lax.rem(me + step, count)
-    found, bit = 0, 1
-    while bit < count:
-        found = found + (((me // bit) % 2 + (step // bit) % 2) % 2) * bit
-        bit *= 2
-    return found
+def block_at(me, step, count):
+    if step == 0:
+        return me
+    far = 1 - 2 * ((2 * me) // count)
+    short = me * ((1 + far) // 2) + (count - 1 - me) * ((1 - far) // 2)
+    half = (step + 1) // 2
+    both = me + far * (half if step % 2 else -half)
+    return jnp.where(step <= 2 * short, both, me + far * (step - short))
 
 
 def layer_kernel(
@@ -60,7 +60,8 @@
     load_down.start()
 
     barrier = pltpu.get_barrier_semaphore()
-    peers = [z_dev(partner_at(ep, s, groups)) for s in range(1, groups)]
+    order = [block_at(ep, s, groups) for s in range(groups)]
+    peers = [z_dev(g) for g in order[1:]]
     peers += [h_dev(at((mine + k) % EXP_DEV, core)) for k in range(1, EXP_DEV)]
     peers += [h_dev(at(mine, (core + j) % shards)) for j in range(1, shards)]
     for dev in peers:
@@ -88,23 +89,36 @@
 
     pl.semaphore_wait(barrier, len(peers))
 
-    def tok_copy(s):
-        g = partner_at(ep, s, groups)
-        return remote(tok_ref, x_all.at[ep], tok_ss.at[s], tok_rs.at[s], z_dev(g))
+    def tok_copy(b, towards):
+        src = x_all.at[b]
+        return remote(src, x_all.at[b], tok_ss.at[b, (towards + 1) // 2], tok_rs.at[b], z_dev(ep + towards))
+
+    def own_tok_copy(towards):
+        return remote(tok_ref, x_all.at[ep], tok_ss.at[ep, (towards + 1) // 2], tok_rs.at[ep], z_dev(ep + towards))
 
     def meta_copy(s):
-        g = partner_at(ep, s, groups)
-        return remote(meta.at[g], meta_in.at[ep], meta_ss.at[s], meta_rs.at[s], z_dev(g))
+        g = order[s]
+        return remote(meta.at[g], meta_in.at[ep], meta_ss.at[s], meta_rs.at[ep], z_dev(g))
+
+    def meta_from(s):
+        g = order[s]
+        return remote(meta.at[g], meta_in.at[g], meta_ss.at[s], meta_rs.at[g], z_dev(g))
+
+    def when_up(fn):
+        pl.when(ep < groups - 1)(fn)
+
+    def when_down(fn):
+        pl.when(ep > 0)(fn)
 
     for s in range(1, groups):
         meta_copy(s).start()
-        tok_copy(s).start()
+    when_up(lambda: own_tok_copy(1).start())
+    when_down(lambda: own_tok_copy(-1).start())
     x_all[ep] = tok_ref[...]
     meta_in[ep] = meta[ep]
 
-    load_up.wait()
-    load_down.wait()
     step_rows = 16
+    pieces = w_gate.shape[0] // step_rows
 
     def split(i, carry):
         r = pl.ds(pl.multiple_of(i * step_rows, step_rows), step_rows)
@@ -112,8 +126,6 @@
         w_up[r, :] = w_pair[r, 1, :]
         return carry
 
-    lax.fori_loop(0, w_gate.shape[0] // step_rows, split, 0)
-
     def row_copy(b, k):
         e = (mine + k) % EXP_DEV
         return remote(r_send.at[b, e], rows.at[b, :, place(hid)], row_ss.at[b, k], row_rs.at[b, k], h_dev(at(e, core)))
@@ -136,18 +148,23 @@
         return remote(y_send.at[b, e], y_in.at[b, mine], y_ss.at[b, k], y_rs.at[b, k], h_dev(at(e, core)))
 
     def z_copy(s):
-        g = partner_at(ep, s, groups)
-        return remote(z_send.at[s], z_in.at[s], z_ss.at[s], z_rs.at[s], z_dev(g))
+        g = order[s]
+        return remote(z_send.at[s], z_in.at[ep], z_ss.at[s], z_rs.at[ep], z_dev(g))
+
+    def z_from(s):
+        g = order[s]
+        return remote(z_send.at[s], z_in.at[g], z_ss.at[s], z_rs.at[g], z_dev(g))
 
     slot_id = lax.broadcasted_iota(jnp.int32, (capacity, tok_rows), 0).astype(jnp.float32)
 
     def stage_rows(s):
-        b = partner_at(ep, s, groups)
-
-        @pl.when(s > 0)
-        def _():
-            meta_copy(s).wait_recv()
-            tok_copy(s).wait_recv()
+        b = order[s]
+
+        if s > 0:
+            meta_from(s).wait_recv()
+            tok_copy(b, 1).wait_recv()
+            pl.when((b < ep) & (ep < groups - 1))(lambda: tok_copy(b, 1).start())
+            pl.when((b > ep) & (ep > 0))(lambda: tok_copy(b, -1).start())
 
         x = x_all[b]
         for e in range(EXP_DEV):
@@ -160,14 +177,14 @@
             fwd_copy(b, 0, j).start()
 
     def stage_forward(s):
-        b = partner_at(ep, s, groups)
+        b = order[s]
         for k in (1, 3, 2):
             row_from(b, k).wait_recv()
             for j in range(1, shards):
                 fwd_copy(b, k, j).start()
 
     def stage_experts(s):
-        b = partner_at(ep, s, groups)
+        b = order[s]
         keep_copy(b).wait()
         for k in range(EXP_DEV):
             for j in range(1, shards):
@@ -187,7 +204,7 @@
             part_copy(b, j).start()
 
     def stage_sum(s):
-        b = partner_at(ep, s, groups)
+        b = order[s]
         for j in range(1, shards):
             part_copy(b, j).wait_recv()
         for e in range(EXP_DEV):
@@ -200,7 +217,7 @@
         y_in[b, mine] = y_send[b, mine]
 
     def stage_mix(s):
-        b = partner_at(ep, s, groups)
+        b = order[s]
         for k in (1, 3, 2):
             y_from(b, k).wait_recv()
         total = jnp.zeros((tok_rows, width), jnp.float32)
@@ -212,12 +229,9 @@
                 spread, y_in[b, e], (((0,), (0,)), ((), ())), preferred_element_type=jnp.float32
             )
 
-        @pl.when(s == 0)
-        def _():
+        if s == 0:
             own[...] = total
-
-        @pl.when(s > 0)
-        def _():
+        else:
             z_send[s] = total.astype(jnp.bfloat16)
             z_copy(s).start()
 
@@ -229,27 +243,33 @@
         e = (mine + EXP_DEV - k) % EXP_DEV
         return remote(r_send.at[b, e], rows.at[b, :, place(at(e, core))], row_ss.at[b, k], row_rs.at[b, k], h_dev(at(e, core)))
 
-    def tick(t, carry):
-        for lag, stage in ((0, stage_rows), (1, stage_forward), (3, stage_sum), (4, stage_mix), (2, stage_experts)):
-            s = t - lag
-
-            @pl.when((s >= 0) & (s < groups))
-            def _():
-                stage(s)
-
-        return carry
-
-    lax.fori_loop(0, groups + 4, tick, 0)
+    load_up.wait()
+    load_down.wait()
+    late = list(range(1, groups)) + [0]
+    for t in range(groups + 5):
+        if t < groups:
+            stage_rows(t)
+        if t < 2:
+            lax.fori_loop(t * (pieces // 2), pieces if t else pieces // 2, split, 0)
+        if 1 <= t <= groups:
+            stage_forward(t - 1)
+        for lag, stage in ((3, stage_sum), (4, stage_mix), (2, stage_experts)):
+            if 0 <= t - lag < groups:
+                stage(late[t - lag])
 
     total = own[...]
     for s in range(1, groups):
-        z_copy(s).wait_recv()
-        total = total + z_in[s].astype(jnp.float32)
+        z_from(s).wait_recv()
+        total = total + z_in[order[s]].astype(jnp.float32)
     out_ref[...] = total.astype(out_ref.dtype)
 
+    when_up(lambda: own_tok_copy(1).wait_send())
+    when_down(lambda: own_tok_copy(-1).wait_send())
     for s in range(1, groups):
+        b = order[s]
         meta_copy(s).wait_send()
-        tok_copy(s).wait_send()
+        pl.when((b < ep) & (ep < groups - 1))(lambda: tok_copy(b, 1).wait_send())
+        pl.when((b > ep) & (ep > 0))(lambda: tok_copy(b, -1).wait_send())
         z_copy(s).wait_send()
 
     def drain(b, carry):
@@ -300,7 +320,7 @@
             pltpu.VMEM((groups, tok_rows, width), bf),
             pltpu.VMEM((tok_rows, width), jnp.float32),
             dma((2,)),
-            dma((groups,)),
+            dma((groups, 2)),
             dma((groups,)),
             dma((groups,)),
             dma((groups,)),

time: 92 us -> 78.7 us (0.86)
  the two profiles are of different devices: /device:TPU:9 before, /device:TPU:0 now
where the time goes in v2:
time: 78.7 us; the launch traced here: 78.5 us
  Pallas kernels  76.9 us (98%)
  local copies, waits for them, and re-layouts  1.67 us (2%)
    pallas_call x1, Pallas kernels, fused_layer(): pl.pallas_call(functools.partial(layer_kernel, groups, hid_count, capacit...  76.9 us
    unnamed x1, local copies, waits for them, and re-layouts  1.67 us

profile of v2, /device:TPU:0, one launch (start us, length us, event | category | flops | bytes accessed | tf_op | source)
XLA Modules:
  0.0 78.5 jit_solution(15025446371849825255)
XLA Ops:
  0.0 76.9 %shard_map.55 = bf16[512,256]{1,0:T(8,128)(2,1)} custom-call(bf16[512,256]{1,0:T(8,128)(2,1)} %tok_ref.1, s32[6,512]{1,0:T(8,128)} %bitcast.6, f32[6,512]{1,0:T(8,128)} %bitcast.7, bf16[704,2,2048]{2,1,0:T(2,128)(2,1)} %bitcast.4, bf16[704,2048]{1,0:T(8,128)(2,1)} %bitcast.5), custom_call_target="tpu_custom_call" | custom-call | tf_op jit(solution)/shard_map/pallas_call | solution.py:300
  76.9 1.7 %copy.7 = bf16[512,256]{1,0:T(8,128)(2,1)} copy(bf16[512,256]{1,0:T(8,128)(2,1)} %shard_map.55) | data formatting | bytes 524288

commit v3 on v2

--- a/solution.py
+++ b/solution.py
@@ -245,17 +245,30 @@
 
     load_up.wait()
     load_down.wait()
-    late = list(range(1, groups)) + [0]
-    for t in range(groups + 5):
-        if t < groups:
-            stage_rows(t)
-        if t < 2:
-            lax.fori_loop(t * (pieces // 2), pieces if t else pieces // 2, split, 0)
-        if 1 <= t <= groups:
-            stage_forward(t - 1)
-        for lag, stage in ((3, stage_sum), (4, stage_mix), (2, stage_experts)):
-            if 0 <= t - lag < groups:
-                stage(late[t - lag])
+    def stage_split(part):
+        lax.fori_loop(part * (pieces // 2), pieces if part else pieces // 2, split, 0)
+
+    last = groups - 1
+    stage_rows(0)
+    stage_split(0)
+    stage_rows(1)
+    stage_split(1)
+    stage_forward(0)
+    for s in range(2, groups):
+        stage_rows(s)
+        stage_forward(s - 1)
+        stage_experts(s - 1)
+        stage_sum(s - 1)
+        if s > 2:
+            stage_mix(s - 2)
+    stage_forward(last)
+    stage_experts(last)
+    stage_sum(last)
+    stage_experts(0)
+    stage_mix(last - 1)
+    stage_sum(0)
+    stage_mix(last)
+    stage_mix(0)
 
     total = own[...]
     for s in range(1, groups):
@@ -395,7 +408,7 @@
 
 def solution(mesh):
     def layer(tokens, *rest):
-        fits = tokens.shape[1] % 128 == 0
+        fits = tokens.shape[1] % 128 == 0 and mesh.shape["ep"] > 2
         return (fused_layer if fits else on_device)(tokens, *rest)
 
     return jax.shard_map(

time: 78.7 us -> 74.6 us (0.948)
  Pallas kernels: 76.9 us -> 72.8 us
    pallas_call x1, Pallas kernels: 76.9 us -> 72.8 us  [fused_layer(): pl.pallas_call(functools.partial(layer_kernel, groups, hid_count, capacit...]
where the time goes in v3:
time: 74.6 us; the launch traced here: 74.5 us
  Pallas kernels  72.8 us (98%)
  local copies, waits for them, and re-layouts  1.67 us (2%)
    pallas_call x1, Pallas kernels, fused_layer(): pl.pallas_call(functools.partial(layer_kernel, groups, hid_count, capacit...  72.8 us
    unnamed x1, local copies, waits for them, and re-layouts  1.67 us

profile of v3, /device:TPU:0, one launch (start us, length us, event | category | flops | bytes accessed | tf_op | source)
XLA Modules:
  0.0 74.5 jit_solution(14513582345676210187)
XLA Ops:
  0.0 72.8 %shard_map.55 = bf16[512,256]{1,0:T(8,128)(2,1)} custom-call(bf16[512,256]{1,0:T(8,128)(2,1)} %tok_ref.1, s32[6,512]{1,0:T(8,128)} %bitcast.6, f32[6,512]{1,0:T(8,128)} %bitcast.7, bf16[704,2,2048]{2,1,0:T(2,128)(2,1)} %bitcast.4, bf16[704,2048]{1,0:T(8,128)(2,1)} %bitcast.5), custom_call_target="tpu_custom_call" | custom-call | tf_op jit(solution)/shard_map/pallas_call | solution.py:313
  72.8 1.7 %copy.7 = bf16[512,256]{1,0:T(8,128)(2,1)} copy(bf16[512,256]{1,0:T(8,128)(2,1)} %shard_map.55) | data formatting | bytes 524288
